TPU v7x, 32 devices: a whole 2x2x4 slice. The times are simulated.
32 devices in a mesh: groups: 2 (over y), tiles: 4 (over z), section: 4 (over x, core).
Axes of the slice: x: 2, y: 2, z: 4, core: 2. Of those that a mesh axis runs over, the one named last changes fastest.
Arguments:
- latents: float32 [4, 192, 8, 128], P('groups', None, 'tiles'), parts along dimension 0, may hold values from -6 to 6
- conv_weight: float32 [4, 27, 192, 192], P('section'), may hold values from -0.078125 to 0.078125
- gain: float32 [4, 192], P('section'), may hold values from 0.1 to 1.9
Outputs:
- decoded: float32 [4, 192, 8, 128], P('groups', 'section', 'tiles'), parts along dimension 0
There are 2 independent parts, one for each index of `groups`. A program takes and returns all parts, laid end to end along the dimension named above; an argument that names none is the same for every part. Nothing has to cross between parts.
All inputs are finite; a program needn't handle non-finite values.
Results may differ from a plain program's by a relative error of at most 0.00013.
Values sent between devices are 32-bit elements; how exact they have to be, the bound alone decides.
No kernel may reach another device: no remote copies, remote signals or barrier semaphores. Data moves between devices by JAX's collectives and lax.ppermute only.
A program may use at most 64 MiB of HBM per device.

v0:
```python
import jax
import jax.numpy as jnp
from jax import lax
from jax.sharding import PartitionSpec as P

EPSILON = 1e-06


def extended(block, sides, width):
    for axis, dim in sides:
        count = lax.axis_size(axis)
        forward = [(i, i + 1) for i in range(count - 1)]
        backward = [(target, source) for source, target in forward]
        low = lax.ppermute(
            lax.slice_in_dim(block, block.shape[dim] - width, None, axis=dim), axis, forward
        )
        high = lax.ppermute(lax.slice_in_dim(block, 0, width, axis=dim), axis, backward)
        block = jnp.concatenate([low, block, high], axis=dim)
    return block


def from_behind(value, axis, by):
    peers = lax.axis_size(axis)
    pairs = [(i, i + by) for i in range(peers) if 0 <= i + by < peers]
    return lax.ppermute(value, axis, pairs)


def broadcast(value, axis, source):
    kept = jnp.where(lax.axis_index(axis) == source, value, 0).astype(value.dtype)
    return lax.psum(kept, axis)


def normalize(values, gain_row):
    meansq = jnp.mean(values * values, axis=1, keepdims=True)
    scaled = values * lax.rsqrt(meansq + EPSILON) * gain_row[None, :, None, None]
    return jax.nn.silu(scaled)


def add_rim(normed):
    return extended(normed, (("tiles", 2),), 1)


def convolve(padded, kernel, block_len, rows_here, col_count):
    summed = jnp.zeros((block_len, kernel.shape[1], rows_here, col_count), jnp.float32)
    for time_off in range(3):
        for row_off in range(3):
            for col_off in range(3):
                window = padded[
                    time_off : time_off + block_len,
                    :,
                    row_off : row_off + rows_here,
                    col_off : col_off + col_count,
                ]
                summed = summed + jnp.einsum(
                    "oi,tirw->torw",
                    kernel[time_off * 9 + row_off * 3 + col_off],
                    window,
                    precision=lax.Precision.HIGHEST,
                )
    return summed


def by_layers(latents, conv_weight, gain):
    kernel = conv_weight[0]
    gain_row = gain[0]
    frame_count, channels, rows_here, col_count = latents.shape
    layer_count = lax.axis_size("section")
    position = lax.axis_index("section")
    block_count = frame_count // frame_count
    step_count = block_count + layer_count - 1
    initial = jnp.zeros((frame_count, channels, rows_here, col_count), jnp.float32)
    memory_init = jnp.zeros((2, channels, rows_here + 2, col_count), jnp.float32)
    results_init = jnp.zeros_like(latents)

    def compute(operand):
        return convolve(operand, kernel, frame_count, rows_here, col_count)

    def skipped(operand):
        return jnp.zeros((frame_count, channels, rows_here, col_count), jnp.float32)

    def advance(step_now, loop_state):
        passing, memory, results = loop_state
        incoming = from_behind(passing, "section", 1)
        block_index = step_now - position
        active = (block_index >= 0) & (block_index < block_count)
        source = jnp.where(position == 0, latents, incoming)
        normed = normalize(source, gain_row)
        with_rim = add_rim(normed)
        joined = jnp.concatenate([memory, with_rim], axis=0)
        padded = jnp.pad(joined, ((0, 0), (0, 0), (0, 0), (1, 1)))
        branch = lax.cond(active, compute, skipped, padded)
        output = source + branch
        memory = jnp.where(active, joined[-2:], memory)
        store_now = active & (position == layer_count - 1)
        results = jnp.where(store_now, output, results)
        return (output, memory, results)

    final_state = lax.fori_loop(0, step_count, advance, (initial, memory_init, results_init))
    gathered = broadcast(final_state[2], "section", layer_count - 1)
    share = channels // layer_count
    return lax.dynamic_slice_in_dim(gathered, position * share, share, 1)


def local(latents, conv_weight, gain):
    return by_layers(latents, conv_weight, gain)


def solution(mesh):
    return jax.shard_map(
        local,
        mesh=mesh,
        in_specs=(
            P("groups", None, "tiles", None),
            P("section", None, None, None),
            P("section", None),
        ),
        out_specs=P("groups", "section", "tiles", None),
        check_vma=False,
    )
```

profile of v0, /device:TPU:0, one launch (start us, length us, event | category | flops | bytes accessed | tf_op | source)
XLA Modules:
  0.0 192.6 jit_solution(15802440383919716907)
XLA Ops:
  7.6 99.6 %while.20 = (s32[]{:T(128)}, f32[2,192,2,128]{3,1,2,0:T(8,128)S(1)}, f32[2,192,4,128]{3,1,2,0:T(8,128)S(1)}, f32[2,192,2,128]{3,1,2,0:T(8,128)S(1)}, pred[]{:T(5...) while((s32[]{:T(128)}, ...), condition=%wide.region_4.5_spmd.clone, body=%wide.region_0.4_spmd.clone.sunk | while | flops 6121095680 | bytes 99492952 | solution.py:98
  7.6 2.4 %collective-permute-start = (f32[2,192,2,128]{3,1,2,0:T(8,128)S(1)}, f32[2,192,2,128]{3,1,2,0:T(8,128)S(1)}, u32[]{:S(2)}, u32[]{:S(2)}) collective-permute-start(f32[2,192,2,128]{3,1,2,0:T(8,128)S(1)} %broadcast_select_fusion.6), channel_id=1, source_target_pairs={{0,1},{1,2},{2,3},{4,5},{5,6},{6,7},{8,9},{9,10},{10,11},{12,13},{... | collective-permute-start | bytes 1179656 | tf_op jit(solution)/shard_map/while/body/eval_jaxpr/ppermute | solution.py:25
  10.0 1.3 collective-permute-done
  12.3 1.3 collective-permute-start.1
  13.6 4.9 %collective-permute-start.2 = (f32[2,192,1,128]{3,1,2,0:T(8,128)S(1)}, f32[2,192,1,128]{3,1,2,0:T(8,128)S(1)}, u32[]{:S(2)}, u32[]{:S(2)}) collective-permute-start(f32[2,192,1,128]{3,1,2,0:T(8,128)S(1)} %get-tuple-element.376), channel_id=1, source_target_pairs={{0,4},{4,8},{8,12},{1,5},{5,9},{9,13},{2,6},{6,10},{10,14},{3,7},{... | collective-permute-start | bytes 589832 | tf_op jit(solution)/shard_map/while/body/eval_jaxpr/ppermute | solution.py:14
  18.6 1.7 collective-permute-done.1
  20.3 1.5 collective-permute-done.2
  22.1 19.5 %conditional.3 = (f32[2,192,2,128]{3,1,2,0:T(8,128)S(1)}) conditional(s32[]{:T(128)} %convert_element_type.22, () %tuple.63, (f32[4,192,4,128]{3,1,2,0:T(8,128)S(1)}, f32[27,192,192]{2,1,0:T(8,128)}) %tuple.64), branch_computations={%region_2.2_spmd, %region_3.3_spmd} | conditional | flops 6117851136 | bytes 84541480 | solution.py:91
  22.1 1.6 fusion.46
  23.8 1.6 convolution_add_fusion.10
  25.4 1.6 convolution_add_fusion.9
  41.9 1.3 collective-permute-start
  43.2 1.3 collective-permute-done
  45.5 1.3 collective-permute-start.1
  46.8 5.0 %collective-permute-start.2 = (f32[2,192,1,128]{3,1,2,0:T(8,128)S(1)}, f32[2,192,1,128]{3,1,2,0:T(8,128)S(1)}, u32[]{:S(2)}, u32[]{:S(2)}) collective-permute-start(f32[2,192,1,128]{3,1,2,0:T(8,128)S(1)} %get-tuple-element.376), channel_id=1, source_target_pairs={{0,4},{4,8},{8,12},{1,5},{5,9},{9,13},{2,6},{6,10},{10,14},{3,7},{... | collective-permute-start | bytes 589832 | tf_op jit(solution)/shard_map/while/body/eval_jaxpr/ppermute | solution.py:14
  51.8 3.5 %collective-permute-done.1 = f32[2,192,1,128]{3,1,2,0:T(8,128)S(1)} collective-permute-done((f32[2,192,1,128]{3,1,2,0:T(8,128)S(1)}, f32[2,192,1,128]{3,1,2,0:T(8,128)S(1)}, u32[]{:S(2)}, u32[]{:S(2)}) %collective-permute-start.1) | collective-permute-done | bytes 196640 | tf_op jit(solution)/shard_map/while/body/eval_jaxpr/ppermute | solution.py:17
  55.3 1.2 collective-permute-done.2
  57.2 20.9 %collective-permute-start = (f32[2,192,2,128]{3,1,2,0:T(8,128)S(1)}, f32[2,192,2,128]{3,1,2,0:T(8,128)S(1)}, u32[]{:S(2)}, u32[]{:S(2)}) collective-permute-start(f32[2,192,2,128]{3,1,2,0:T(8,128)S(1)} %broadcast_select_fusion.6), channel_id=1, source_target_pairs={{0,1},{1,2},{2,3},{4,5},{5,6},{6,7},{8,9},{9,10},{10,11},{12,13},{... | collective-permute-start | bytes 1179656 | tf_op jit(solution)/shard_map/while/body/eval_jaxpr/ppermute | solution.py:25
  78.1 1.3 collective-permute-done
  80.4 1.3 collective-permute-start.1
  81.7 5.0 %collective-permute-start.2 = (f32[2,192,1,128]{3,1,2,0:T(8,128)S(1)}, f32[2,192,1,128]{3,1,2,0:T(8,128)S(1)}, u32[]{:S(2)}, u32[]{:S(2)}) collective-permute-start(f32[2,192,1,128]{3,1,2,0:T(8,128)S(1)} %get-tuple-element.376), channel_id=1, source_target_pairs={{0,4},{4,8},{8,12},{1,5},{5,9},{9,13},{2,6},{6,10},{10,14},{3,7},{... | collective-permute-start | bytes 589832 | tf_op jit(solution)/shard_map/while/body/eval_jaxpr/ppermute | solution.py:14
  86.7 1.7 collective-permute-done.1
  88.4 1.5 collective-permute-done.2
  90.5 4.5 %collective-permute-start = (f32[2,192,2,128]{3,1,2,0:T(8,128)S(1)}, f32[2,192,2,128]{3,1,2,0:T(8,128)S(1)}, u32[]{:S(2)}, u32[]{:S(2)}) collective-permute-start(f32[2,192,2,128]{3,1,2,0:T(8,128)S(1)} %broadcast_select_fusion.6), channel_id=1, source_target_pairs={{0,1},{1,2},{2,3},{4,5},{5,6},{6,7},{8,9},{9,10},{10,11},{12,13},{... | collective-permute-start | bytes 1179656 | tf_op jit(solution)/shard_map/while/body/eval_jaxpr/ppermute | solution.py:25
  95.0 1.3 collective-permute-done
  97.3 1.3 collective-permute-start.1
  98.6 4.7 %collective-permute-start.2 = (f32[2,192,1,128]{3,1,2,0:T(8,128)S(1)}, f32[2,192,1,128]{3,1,2,0:T(8,128)S(1)}, u32[]{:S(2)}, u32[]{:S(2)}) collective-permute-start(f32[2,192,1,128]{3,1,2,0:T(8,128)S(1)} %get-tuple-element.376), channel_id=1, source_target_pairs={{0,4},{4,8},{8,12},{1,5},{5,9},{9,13},{2,6},{6,10},{10,14},{3,7},{... | collective-permute-start | bytes 589832 | tf_op jit(solution)/shard_map/while/body/eval_jaxpr/ppermute | solution.py:14
  103.3 1.7 collective-permute-done.1
  105.0 1.5 collective-permute-done.2
  107.1 1.1 copy_select_fusion
  108.3 76.0 %all-reduce.3.cloned.1.call-done = f32[2,192,2,128]{3,2,1,0:T(2,128)} async-done(((f32[2,192,2,128]{3,2,1,0:T(2,128)}), f32[2,192,2,128]{3,2,1,0:T(2,128)}) %all-reduce.3.cloned.1.call-update) | async-done | bytes 393232 | tf_op jit(solution)/shard_map/psum | solution.py:30
  184.2 1.5 constant_dynamic-slice_fusion
  (70 shorter events, 22.0 us)
Async XLA Ops:
  6.5 177.7 %all-reduce.3.cloned.1.call-start = ((), (), s32[]{:S(2)}) async-start(), calls=%async_computation | async-start | bytes 786432 | tf_op jit(solution)/shard_map/psum | solution.py:30
  7.6 3.7 %collective-permute-start = (f32[2,192,2,128]{3,1,2,0:T(8,128)S(1)}, f32[2,192,2,128]{3,1,2,0:T(8,128)S(1)}, u32[]{:S(2)}, u32[]{:S(2)}) collective-permute-start(f32[2,192,2,128]{3,1,2,0:T(8,128)S(1)} %broadcast_select_fusion.6), channel_id=1, source_target_pairs={{0,1},{1,2},{2,3},{4,5},{5,6},{6,7},{8,9},{9,10},{10,11},{12,13},{... | collective-permute-start | bytes 1179656 | tf_op jit(solution)/shard_map/while/body/eval_jaxpr/ppermute | solution.py:25
  12.3 7.9 %collective-permute-start.1 = (f32[2,192,1,128]{3,1,2,0:T(8,128)S(1)}, f32[2,192,1,128]{3,1,2,0:T(8,128)S(1)}, u32[]{:S(2)}, u32[]{:S(2)}) collective-permute-start(f32[2,192,1,128]{3,1,2,0:T(8,128)S(1)} %get-tuple-element.375), channel_id=1, source_target_pairs={{4,0},{8,4},{12,8},{5,1},{9,5},{13,9},{6,2},{10,6},{14,10},{7,3},{... | collective-permute-start | bytes 589832 | tf_op jit(solution)/shard_map/while/body/eval_jaxpr/ppermute | solution.py:17
  13.6 8.1 %collective-permute-start.2 = (f32[2,192,1,128]{3,1,2,0:T(8,128)S(1)}, f32[2,192,1,128]{3,1,2,0:T(8,128)S(1)}, u32[]{:S(2)}, u32[]{:S(2)}) collective-permute-start(f32[2,192,1,128]{3,1,2,0:T(8,128)S(1)} %get-tuple-element.376), channel_id=1, source_target_pairs={{0,4},{4,8},{8,12},{1,5},{5,9},{9,13},{2,6},{6,10},{10,14},{3,7},{... | collective-permute-start | bytes 589832 | tf_op jit(solution)/shard_map/while/body/eval_jaxpr/ppermute | solution.py:14
  22.1 4.8 %copy-start = (f32[27,192,192]{2,1,0:T(8,128)S(1)}, f32[27,192,192]{2,1,0:T(8,128)}, u32[]{:S(2)}) copy-start(f32[27,192,192]{2,1,0:T(8,128)} %get-tuple-element.219) | copy-start | bytes 11943940 | tf_op jit(solution)/shard_map/while/body/eval_jaxpr/cond
  41.9 2.6 %collective-permute-start = (f32[2,192,2,128]{3,1,2,0:T(8,128)S(1)}, f32[2,192,2,128]{3,1,2,0:T(8,128)S(1)}, u32[]{:S(2)}, u32[]{:S(2)}) collective-permute-start(f32[2,192,2,128]{3,1,2,0:T(8,128)S(1)} %broadcast_select_fusion.6), channel_id=1, source_target_pairs={{0,1},{1,2},{2,3},{4,5},{5,6},{6,7},{8,9},{9,10},{10,11},{12,13},{... | collective-permute-start | bytes 1179656 | tf_op jit(solution)/shard_map/while/body/eval_jaxpr/ppermute | solution.py:25
  45.5 9.8 %collective-permute-start.1 = (f32[2,192,1,128]{3,1,2,0:T(8,128)S(1)}, f32[2,192,1,128]{3,1,2,0:T(8,128)S(1)}, u32[]{:S(2)}, u32[]{:S(2)}) collective-permute-start(f32[2,192,1,128]{3,1,2,0:T(8,128)S(1)} %get-tuple-element.375), channel_id=1, source_target_pairs={{4,0},{8,4},{12,8},{5,1},{9,5},{13,9},{6,2},{10,6},{14,10},{7,3},{... | collective-permute-start | bytes 589832 | tf_op jit(solution)/shard_map/while/body/eval_jaxpr/ppermute | solution.py:17
  46.8 9.7 %collective-permute-start.2 = (f32[2,192,1,128]{3,1,2,0:T(8,128)S(1)}, f32[2,192,1,128]{3,1,2,0:T(8,128)S(1)}, u32[]{:S(2)}, u32[]{:S(2)}) collective-permute-start(f32[2,192,1,128]{3,1,2,0:T(8,128)S(1)} %get-tuple-element.376), channel_id=1, source_target_pairs={{0,4},{4,8},{8,12},{1,5},{5,9},{9,13},{2,6},{6,10},{10,14},{3,7},{... | collective-permute-start | bytes 589832 | tf_op jit(solution)/shard_map/while/body/eval_jaxpr/ppermute | solution.py:14
  57.2 22.2 %collective-permute-start = (f32[2,192,2,128]{3,1,2,0:T(8,128)S(1)}, f32[2,192,2,128]{3,1,2,0:T(8,128)S(1)}, u32[]{:S(2)}, u32[]{:S(2)}) collective-permute-start(f32[2,192,2,128]{3,1,2,0:T(8,128)S(1)} %broadcast_select_fusion.6), channel_id=1, source_target_pairs={{0,1},{1,2},{2,3},{4,5},{5,6},{6,7},{8,9},{9,10},{10,11},{12,13},{... | collective-permute-start | bytes 1179656 | tf_op jit(solution)/shard_map/while/body/eval_jaxpr/ppermute | solution.py:25
  80.4 8.0 %collective-permute-start.1 = (f32[2,192,1,128]{3,1,2,0:T(8,128)S(1)}, f32[2,192,1,128]{3,1,2,0:T(8,128)S(1)}, u32[]{:S(2)}, u32[]{:S(2)}) collective-permute-start(f32[2,192,1,128]{3,1,2,0:T(8,128)S(1)} %get-tuple-element.375), channel_id=1, source_target_pairs={{4,0},{8,4},{12,8},{5,1},{9,5},{13,9},{6,2},{10,6},{14,10},{7,3},{... | collective-permute-start | bytes 589832 | tf_op jit(solution)/shard_map/while/body/eval_jaxpr/ppermute | solution.py:17
  81.7 8.2 %collective-permute-start.2 = (f32[2,192,1,128]{3,1,2,0:T(8,128)S(1)}, f32[2,192,1,128]{3,1,2,0:T(8,128)S(1)}, u32[]{:S(2)}, u32[]{:S(2)}) collective-permute-start(f32[2,192,1,128]{3,1,2,0:T(8,128)S(1)} %get-tuple-element.376), channel_id=1, source_target_pairs={{0,4},{4,8},{8,12},{1,5},{5,9},{9,13},{2,6},{6,10},{10,14},{3,7},{... | collective-permute-start | bytes 589832 | tf_op jit(solution)/shard_map/while/body/eval_jaxpr/ppermute | solution.py:14
  90.5 5.8 %collective-permute-start = (f32[2,192,2,128]{3,1,2,0:T(8,128)S(1)}, f32[2,192,2,128]{3,1,2,0:T(8,128)S(1)}, u32[]{:S(2)}, u32[]{:S(2)}) collective-permute-start(f32[2,192,2,128]{3,1,2,0:T(8,128)S(1)} %broadcast_select_fusion.6), channel_id=1, source_target_pairs={{0,1},{1,2},{2,3},{4,5},{5,6},{6,7},{8,9},{9,10},{10,11},{12,13},{... | collective-permute-start | bytes 1179656 | tf_op jit(solution)/shard_map/while/body/eval_jaxpr/ppermute | solution.py:25
  97.3 7.7 %collective-permute-start.1 = (f32[2,192,1,128]{3,1,2,0:T(8,128)S(1)}, f32[2,192,1,128]{3,1,2,0:T(8,128)S(1)}, u32[]{:S(2)}, u32[]{:S(2)}) collective-permute-start(f32[2,192,1,128]{3,1,2,0:T(8,128)S(1)} %get-tuple-element.375), channel_id=1, source_target_pairs={{4,0},{8,4},{12,8},{5,1},{9,5},{13,9},{6,2},{10,6},{14,10},{7,3},{... | collective-permute-start | bytes 589832 | tf_op jit(solution)/shard_map/while/body/eval_jaxpr/ppermute | solution.py:17
  98.6 7.9 %collective-permute-start.2 = (f32[2,192,1,128]{3,1,2,0:T(8,128)S(1)}, f32[2,192,1,128]{3,1,2,0:T(8,128)S(1)}, u32[]{:S(2)}, u32[]{:S(2)}) collective-permute-start(f32[2,192,1,128]{3,1,2,0:T(8,128)S(1)} %get-tuple-element.376), channel_id=1, source_target_pairs={{0,4},{4,8},{8,12},{1,5},{5,9},{9,13},{2,6},{6,10},{10,14},{3,7},{... | collective-permute-start | bytes 589832 | tf_op jit(solution)/shard_map/while/body/eval_jaxpr/ppermute | solution.py:14
Sparse Core Ops, SparseCore 0:
  108.4 75.7 all-reduce.2
where the time goes:
time: 193 us
  waiting for transfers between devices  95.3 us (49%)
  starting transfers between devices  54 us (28%)
  matrix products  19.3 us (10%)
  between operations  13.4 us (7%)
  other arithmetic  7.2 us (4%)
  local copies, waits for them, and re-layouts  2.76 us (1%)
    psum x1, waiting for transfers between devices, broadcast(): return lax.psum(kept, axis)  76 us
    ppermute x4, starting transfers between devices, from_behind(): return lax.ppermute(value, axis, pairs)  29.1 us
    ppermute x4, starting transfers between devices, extended(): lax.ppermute(lax.slice_in_dim(block, block.shape[dim] - width, None, axis...  19.7 us
    dot_general x27, matrix products, convolve(): jnp.einsum('oi,tirw->torw', kernel[time_off * 9 + row_off * 3 + col_off],...  19.3 us
    ppermute x4, waiting for transfers between devices, extended(): lax.ppermute(lax.slice_in_dim(block, 0, width, axis=dim), axis, backward)  8.53 us
    ppermute x4, waiting for transfers between devices, extended(): lax.ppermute(lax.slice_in_dim(block, block.shape[dim] - width, None, axis...  5.56 us
    ppermute x4, waiting for transfers between devices, from_behind(): return lax.ppermute(value, axis, pairs)  5.23 us
    ppermute x4, starting transfers between devices, extended(): lax.ppermute(lax.slice_in_dim(block, 0, width, axis=dim), axis, backward)  5.17 us
  transfers between devices with their start and end apart: 13, of which 13 were waited for; matrix products, arithmetic and copies ran while one was open for 0% of the time, Pallas kernels for 0%

commit v1 on v0

v1 whole, which is shorter than its diff:
```python
import jax
import jax.numpy as jnp
from jax import lax
from jax.experimental import pallas as pl
from jax.experimental.pallas import tpu as pltpu
from jax.sharding import PartitionSpec as P

EPSILON = 1e-06
VMEM = pl.BlockSpec(memory_space=pltpu.VMEM)
ANY = pl.BlockSpec(memory_space=pl.ANY)


def partner_a(tile, tiles):
    other = tile ^ 1
    return other if other < tiles else tile


def partner_b(tile, tiles):
    other = ((tile - 1) ^ 1) + 1 if tile > 0 else tile
    return other if other < tiles else tile


def idle_cycle(where, names):
    for k, name in enumerate(names):
        where[name] = names[(k + 1) % len(names)]


def section_hop(layer, sections):
    where = {}
    if layer % 2 == 0:
        idle_cycle(where, [layer, layer + 1])
    elif layer + 2 < sections:
        idle_cycle(where, [layer - 1, layer, layer + 1, layer + 2])
    else:
        idle_cycle(where, [layer - 1, layer, layer + 1])
    taken = set(where)
    for s in range(sections):
        if s not in taken:
            where[s] = s ^ 1 if (s ^ 1) not in taken and (s ^ 1) < sections else s
    return where


def hop_pairs(layer, tiles, sections, tile_of):
    hop = section_hop(layer, sections)
    pairs = []
    for t in range(tiles):
        for s in range(sections):
            goal = tile_of(t) if s == layer else t
            pairs.append((t * sections + s, goal * sections + hop[s]))
    return pairs


def rim_pairs(tiles, sections, tile_of):
    pairs = []
    for t in range(tiles):
        where = {}
        if tile_of(t) == t:
            for s in range(sections):
                where[s] = s ^ 1 if (s ^ 1) < sections else s
        else:
            idle_cycle(where, list(range(1, sections)))
        for s in range(sections):
            if s == 0 and tile_of(t) != t:
                pairs.append((t * sections, tile_of(t) * sections))
            else:
                pairs.append((t * sections + s, t * sections + where[s]))
    return pairs


def share_pairs(target, tiles, sections):
    last = sections - 1
    where = {}
    if target == last - 1 or (target ^ 1) >= last - 1:
        idle_cycle(where, [last, target])
    else:
        idle_cycle(where, [last, target, target ^ 1, last - 1])
    taken = set(where)
    for s in range(sections):
        if s not in taken:
            where[s] = s ^ 1 if (s ^ 1) not in taken and (s ^ 1) < sections else s
    return [
        (t * sections + s, t * sections + where[s])
        for t in range(tiles)
        for s in range(sections)
    ]


def send(value, pairs):
    return lax.ppermute(value, ("tiles", "section"), pairs)


def split(values):
    high = values.astype(jnp.bfloat16)
    low = (values - high.astype(jnp.float32)).astype(jnp.bfloat16)
    return high, low


def prepare_kernel(first, depth, weight, high, low, staged, sems):
    count, channels = staged.shape[0], staged.shape[1]
    copies = []
    for k in range(count):
        copies.append(
            pltpu.make_async_copy(weight.at[first + k], staged.at[k], sems.at[k])
        )
        copies[-1].start()
    for a in range(count // 9):
        for k in range(0, 9, 2):
            copies[9 * a + k].wait()
            parts = [staged[9 * a + k]]
            if k + 1 < 9:
                copies[9 * a + k + 1].wait()
                parts.append(staged[9 * a + k + 1])
                width = 2 * channels
            else:
                width = depth - 8 * channels
                if width > channels:
                    parts.append(jnp.zeros((channels, width - channels), jnp.float32))
            block = jnp.concatenate(parts, axis=1)
            upper, lower = split(block)
            high[a, :, k * channels : k * channels + width] = upper
            low[a, :, k * channels : k * channels + width] = lower


def prepare(weight, steps, depth):
    channels = weight.shape[1]
    shape = jax.ShapeDtypeStruct((steps, channels, depth), jnp.bfloat16)

    def kernel(*refs):
        prepare_kernel(9 * (3 - steps), depth, *refs)

    return pl.pallas_call(
        kernel,
        out_shape=(shape, shape),
        in_specs=[ANY],
        out_specs=(VMEM, VMEM),
        scratch_shapes=[
            pltpu.VMEM((9 * steps, channels, channels), jnp.float32),
            pltpu.SemaphoreType.DMA((9 * steps,)),
        ],
        name="prepare",
    )(weight)


def normalize(values, gain):
    meansq = jnp.mean(values * values, axis=0, keepdims=True)
    scaled = values * lax.rsqrt(meansq + EPSILON) * gain
    return scaled / (1.0 + jnp.exp(-scaled))


def shifted(values, col_off):
    if col_off == 1:
        return values
    width = values.shape[1]
    lane = lax.broadcasted_iota(jnp.int32, values.shape, 1)
    if col_off == 0:
        return jnp.where(lane == 0, 0.0, pltpu.roll(values, 1, 1))
    return jnp.where(lane == width - 1, 0.0, pltpu.roll(values, width - 1, 1))


def product(high, low, patch_high, patch_low):
    def dot(a, b):
        return jnp.dot(a, b, preferred_element_type=jnp.float32)

    return dot(high, patch_high) + dot(low, patch_high) + dot(high, patch_low)


def frame_step(layer, tiles, main, near_a, near_b, gain, weights, partial, keep):
    channels, width = near_a.shape
    rows = main.shape[0] // channels
    steps, _, depth = weights[0].shape
    block = jax.ShapeDtypeStruct(main.shape, jnp.float32)
    edge = jax.ShapeDtypeStruct(near_a.shape, jnp.float32)
    patch = jax.ShapeDtypeStruct((depth, rows * width), jnp.bfloat16)

    def kernel(*refs):
        main_ref, a_ref, b_ref, gain_ref, high_ref, low_ref = refs[:6]
        refs = refs[6:]
        if partial is not None:
            partial_ref, refs = refs[0], refs[1:]
        out_ref, out_a_ref, out_b_ref, patch_high, patch_low = refs
        tile = lax.axis_index("tiles")
        even = lax.rem(tile, 2) == 0

        @pl.when(lax.axis_index("section") == layer)
        def _():
            gains = gain_ref[...]
            near_one, near_two = a_ref[...], b_ref[...]
            above = jnp.where(even, near_two, near_one)
            below = jnp.where(even, near_one, near_two)
            above = jnp.where(tile == 0, 0.0, above)
            below = jnp.where(tile == tiles - 1, 0.0, below)
            own = [main_ref[r * channels : (r + 1) * channels, :] for r in range(rows)]
            if depth > 9 * channels:
                pad = jnp.zeros((depth - 9 * channels, rows * width), jnp.bfloat16)
                patch_high[9 * channels :, :] = pad
                patch_low[9 * channels :, :] = pad
            for q, source in enumerate([above] + own + [below]):
                normed = normalize(source, gains)
                for e in range(3):
                    upper, lower = split(shifted(normed, e))
                    for b in range(3):
                        r = q - b
                        if 0 <= r < rows:
                            k = (3 * b + e) * channels
                            cols = slice(r * width, (r + 1) * width)
                            patch_high[k : k + channels, cols] = upper
                            patch_low[k : k + channels, cols] = lower
            total = product(
                high_ref[steps - 1], low_ref[steps - 1], patch_high[...], patch_low[...]
            )
            if partial is not None:
                total = total + partial_ref[...]
            results = [
                own[r] + total[:, r * width : (r + 1) * width] for r in range(rows)
            ]
            for r in range(rows):
                out_ref[r * channels : (r + 1) * channels, :] = results[r]
            out_a_ref[...] = jnp.where(even, results[-1], results[0])
            out_b_ref[...] = jnp.where(even, results[0], results[-1])

    operands = [main, near_a, near_b, gain, *weights]
    if partial is not None:
        operands.append(partial)
    flops = 6 * channels * depth * rows * width
    out_shape = [block, edge, edge]
    scratch = []
    if keep:
        out_shape += [patch, patch]
    else:
        scratch = [pltpu.VMEM(patch.shape, patch.dtype)] * 2
    return pl.pallas_call(
        kernel,
        out_shape=tuple(out_shape),
        in_specs=[VMEM] * len(operands),
        out_specs=tuple([VMEM] * len(out_shape)),
        scratch_shapes=scratch,
        cost_estimate=pl.CostEstimate(
            flops=flops, bytes_accessed=2**20, transcendentals=0
        ),
        name="frame_step",
    )(*operands)


def earlier_frames(layer, weights, patches):
    steps, channels, depth = weights[0].shape
    count = len(patches)
    columns = patches[0][0].shape[1]

    def kernel(high_ref, low_ref, *refs):
        out_ref = refs[-1]

        @pl.when(lax.axis_index("section") == layer)
        def _():
            total = None
            for n in range(count):
                a = steps - 1 - (count - n)
                term = product(
                    high_ref[a], low_ref[a], refs[2 * n][...], refs[2 * n + 1][...]
                )
                total = term if total is None else total + term
            out_ref[...] = total

    operands = [*weights]
    for pair in patches:
        operands += list(pair)
    return pl.pallas_call(
        kernel,
        out_shape=jax.ShapeDtypeStruct((channels, columns), jnp.float32),
        in_specs=[VMEM] * len(operands),
        out_specs=VMEM,
        cost_estimate=pl.CostEstimate(
            flops=6 * channels * depth * columns * count,
            bytes_accessed=2**20,
            transcendentals=0,
        ),
        name="earlier_frames",
    )(*operands)


def local(latents, conv_weight, gain):
    frames, channels, rows, width = latents.shape
    tiles, sections = lax.axis_size("tiles"), lax.axis_size("section")
    tile, section = lax.axis_index("tiles"), lax.axis_index("section")
    depth = -(-9 * channels // 256) * 256
    steps = min(frames, 3)
    of_a = lambda t: partner_a(t, tiles)
    of_b = lambda t: partner_b(t, tiles)

    even = lax.rem(tile, 2) == 0
    by_row = jnp.transpose(latents, (0, 2, 1, 3))
    main = [by_row[f].reshape(rows * channels, width) for f in range(frames)]
    edge_a = [jnp.where(even, by_row[f, -1], by_row[f, 0]) for f in range(frames)]
    edge_b = [jnp.where(even, by_row[f, 0], by_row[f, -1]) for f in range(frames)]
    rim_a, rim_b = (rim_pairs(tiles, sections, of) for of in (of_a, of_b))
    near_a = [send(edge_a[f], rim_a) for f in range(frames)]
    near_b = [send(edge_b[f], rim_b) for f in range(frames)]
    weights = prepare(conv_weight[0], steps, depth)
    gains = gain.reshape(channels, 1)

    for layer in range(sections):
        if layer > 0:
            straight = hop_pairs(layer - 1, tiles, sections, lambda t: t)
            cross_a = hop_pairs(layer - 1, tiles, sections, of_a)
            cross_b = hop_pairs(layer - 1, tiles, sections, of_b)
            main = [send(value, straight) for value in main]
            near_a = [send(value, cross_a) for value in edge_a]
            near_b = [send(value, cross_b) for value in edge_b]
        patches, next_main, edge_a, edge_b = [], [], [], []
        for f in range(frames):
            partial = None
            if f > 0:
                partial = earlier_frames(layer, weights, patches[-2:])
            keep = f < frames - 1
            done = frame_step(
                layer, tiles, main[f], near_a[f], near_b[f], gains, weights, partial, keep
            )
            next_main.append(done[0])
            edge_a.append(done[1])
            edge_b.append(done[2])
            if keep:
                patches.append(done[3:])
        main = next_main

    share = channels // sections
    outs = []
    for f in range(frames):
        cube = main[f].reshape(rows, channels, width)
        own = cube[:, (sections - 1) * share :]
        for target in range(sections - 1):
            part = cube[:, target * share : (target + 1) * share]
            got = send(
                part.reshape(rows * share, width), share_pairs(target, tiles, sections)
            )
            own = jnp.where(section == target, got.reshape(rows, share, width), own)
        outs.append(own)
    return jnp.transpose(jnp.stack(outs), (0, 2, 1, 3))


def solution(mesh):
    return jax.shard_map(
        local,
        mesh=mesh,
        in_specs=(
            P("groups", None, "tiles", None),
            P("section", None, None, None),
            P("section", None),
        ),
        out_specs=P("groups", "section", "tiles", None),
        check_vma=False,
    )
```

time: 193 us -> 86.2 us (0.45)
  waiting for transfers between devices: 95.3 us -> 2.74 us
  Pallas kernels: 0 us -> 43.3 us
  starting transfers between devices: 54 us -> 25.4 us
  matrix products: 19.3 us -> 0 us
  between operations: 13.4 us -> 0.23 us
  local copies, waits for them, and re-layouts: 2.76 us -> 13.3 us
  other arithmetic: 7.2 us -> 0.87 us
    psum x1 -> x0, waiting for transfers between devices: 76 us -> none  [broadcast(): return lax.psum(kept, axis)]
    pallas_call x0 -> x13, Pallas kernels: none -> 43.3 us  [the longest x8 26.8 us: frame_step(): pl.pallas_call(kernel, out_shape=tuple(out_shape), in_specs=[VMEM] * len(...]
    ppermute x12 -> x28, starting transfers between devices: 53.9 us -> 25.4 us  [send(): return lax.ppermute(value, ('tiles', 'section'), pairs)]
    dot_general x27 -> x0, matrix products: 19.3 us -> none  [convolve(): jnp.einsum('oi,tirw->torw', kernel[time_off * 9 + row_off * 3 + col_off],...]
    ppermute x12 -> x28, waiting for transfers between devices: 19.3 us -> 2.74 us  [send(): return lax.ppermute(value, ('tiles', 'section'), pairs)]
    unnamed x1 -> x53, local copies, waits for them, and re-layouts: 1.02 us -> 10.2 us
    mul x4 -> x0, other arithmetic: 3.43 us -> none  [normalize(): return jax.nn.silu(scaled)]
    select_n x9 -> x1, other arithmetic: 2.89 us -> 0.03 us  [local(): jnp.where(even, by_row[f, 0], by_row[f, -1])]
  transfers between devices with their start and end apart: 13 -> 28, of which waited for: 13 -> 2; matrix products, arithmetic and copies ran while one was open for 0% -> 3% of each run, Pallas kernels for 0% -> 47%
where the time goes in v1:
time: 86.2 us; the launch traced here: 85.8 us
  Pallas kernels  43.3 us (50%)
  starting transfers between devices  25.4 us (29%)
  local copies, waits for them, and re-layouts  13.3 us (15%)
  waiting for transfers between devices  2.74 us (3%)
  other arithmetic  0.87 us (1%)
    pallas_call x8, Pallas kernels, frame_step(): pl.pallas_call(kernel, out_shape=tuple(out_shape), in_specs=[VMEM] * len(...  26.8 us
    ppermute x28, starting transfers between devices, send(): return lax.ppermute(value, ('tiles', 'section'), pairs)  25.4 us
    pallas_call x4, Pallas kernels, earlier_frames(): pl.pallas_call(kernel, out_shape=jax.ShapeDtypeStruct((channels, columns)...  12.7 us
    unnamed x53, local copies, waits for them, and re-layouts  10.2 us
    pallas_call x1, Pallas kernels, prepare(): pl.pallas_call(kernel, out_shape=(shape, shape), in_specs=[ANY], out_spec...  3.87 us
    ppermute x28, waiting for transfers between devices, send(): return lax.ppermute(value, ('tiles', 'section'), pairs)  2.74 us
  transfers between devices with their start and end apart: 28, of which 2 were waited for; matrix products, arithmetic and copies ran while one was open for 3% of the time, Pallas kernels for 47%

profile of v1, /device:TPU:0, one launch (start us, length us, event | category | flops | bytes accessed | tf_op | source)
XLA Modules:
  0.0 85.8 jit_solution(1492552237268661428)
XLA Ops:
  0.0 1.0 %copy.18 = f32[2,192,2,128]{3,1,2,0:T(8,128)S(1)} copy(f32[2,192,2,128]{3,2,1,0:T(2,128)} %param.3) | data formatting | bytes 786432 | tf_op args[0]
  1.1 3.1 %collective-permute-start.14 = (f32[192,128]{1,0:T(8,128)S(1)}, f32[192,128]{1,0:T(8,128)S(1)}, u32[]{:S(2)}, u32[]{:S(2)}) collective-permute-start(f32[192,128]{1,0:T(8,128)S(1)} %get-tuple-element.66), channel_id=1, source_target_pairs={{0,4},{1,2},{2,3},{3,1},{4,0},{5,6},{6,7},{7,5},{8,12},{9,10},{10,... | collective-permute-start | bytes 294920 | tf_op jit(solution)/shard_map/ppermute | solution.py:89
  4.2 3.1 %collective-permute-start = (f32[192,128]{1,0:T(8,128)S(1)}, f32[192,128]{1,0:T(8,128)S(1)}, u32[]{:S(2)}, u32[]{:S(2)}) collective-permute-start(f32[192,128]{1,0:T(8,128)S(1)} %get-tuple-element.68), channel_id=1, source_target_pairs={{0,4},{1,2},{2,3},{3,1},{4,0},{5,6},{6,7},{7,5},{8,12},{9,10},{10,... | collective-permute-start | bytes 294920 | tf_op jit(solution)/shard_map/ppermute | solution.py:89
  7.4 0.8 fusion.6
  8.1 0.8 copy.8.refs_3_
  8.9 3.9 %prepare.1 = (bf16[2,192,1792]{2,1,0:T(8,128)(2,1)}, bf16[2,192,1792]{2,1,0:T(8,128)(2,1)}) custom-call(f32[27,192,192]{2,1,0:T(8,128)} %bitcast.35), custom_call_target="tpu_custom_call" | custom-call | tf_op jit(solution)/shard_map/prepare/pallas_call | solution.py:131
  13.5 4.5 %frame_step.8 = (f32[384,128]{1,0:T(8,128)}, f32[192,128]{1,0:T(8,128)}, f32[192,128]{1,0:T(8,128)}, bf16[1792,256]{1,0:T(8,128)(2,1)}, bf16[1792,256]{1,0:T(8,128)(2,1)}) custom-call(f32[384,128]{1,0:T(8,128)} %bitcast.38, f32[192,128]{1,0:T(8,128)} %copy-done.13, f32[192,128]{1,0:T(8,128)} %copy-done.14, f32[192,1]{1,0:T(8,128)} %copy.8.refs_3_, ...), custom_call_target="tpu_custom_call" | custom-call | flops 528482304 | bytes 1048576 | tf_op jit(solution)/shard_map/frame_step/pallas_call | solution.py:231
  18.0 1.7 %collective-permute-start.3 = (f32[192,128]{1,0:T(8,128)}, f32[192,128]{1,0:T(8,128)S(1)}, u32[]{:S(2)}, u32[]{:S(2)}) collective-permute-start(f32[192,128]{1,0:T(8,128)} %get-tuple-element.38), channel_id=1, source_target_pairs={{0,5},{1,0},{2,3},{3,2},{4,1},{5,4},{6,7},{7,6},{8,13},{9,8},{10,1... | collective-permute-start | bytes 294920 | tf_op jit(solution)/shard_map/ppermute | solution.py:89
  19.7 3.7 %earlier_frames.4.refs_6_ = f32[192,256]{1,0:T(8,128)} custom-call(bf16[2,192,1792]{2,1,0:T(8,128)(2,1)} %get-tuple-element.35.refs_4_.high_ref, bf16[2,192,1792]{2,1,0:T(8,128)(2,1)} %get-tuple-element.36.refs_5_.low_ref, bf16[1792,256]{1,0:T(8,128)(2,1)} %get-tuple-element.47.refs_0_, bf16[1792,256]{1,0:T(8,128)(2,1)} %get-tuple-element.48.refs_1_), custom_call_target="tpu_custom_call" | custom-call | flops 528482304 | bytes 1048576 | tf_op jit(solution)/shard_map/earlier_frames/pallas_call | solution.py:266
  24.1 3.8 %frame_step.12 = (f32[384,128]{1,0:T(8,128)}, f32[192,128]{1,0:T(8,128)}, f32[192,128]{1,0:T(8,128)}) custom-call(f32[384,128]{1,0:T(8,128)} %bitcast.39, f32[192,128]{1,0:T(8,128)} %copy-done.15, f32[192,128]{1,0:T(8,128)} %copy-done.16, f32[192,1]{1,0:T(8,128)} %copy.8.refs_3_, bf16[2,192,1792]{2,1,0:T(8,128)(2,1)} %get-tuple-element.35.refs_4_.high_ref, ...), custom_call_target="tpu_custom_call" | custom-call | flops 528482304 | bytes 1048576 | tf_op jit(solution)/shard_map/frame_step/pallas_call | solution.py:231
  29.1 0.7 copy-done.2
  29.8 3.4 %frame_step.9 = (f32[384,128]{1,0:T(8,128)}, f32[192,128]{1,0:T(8,128)}, f32[192,128]{1,0:T(8,128)}, bf16[1792,256]{1,0:T(8,128)(2,1)}, bf16[1792,256]{1,0:T(8,128)(2,1)}) custom-call(f32[384,128]{1,0:T(8,128)} %copy-done.2, f32[192,128]{1,0:T(8,128)} %copy-done.10, f32[192,128]{1,0:T(8,128)} %copy-done.11, f32[192,1]{1,0:T(8,128)} %copy.8.refs_3_, ...), custom_call_target="tpu_custom_call" | custom-call | flops 528482304 | bytes 1048576 | tf_op jit(solution)/shard_map/frame_step/pallas_call | solution.py:231
  33.2 1.6 %collective-permute-start.5 = (f32[384,128]{1,0:T(8,128)}, f32[384,128]{1,0:T(8,128)S(1)}, u32[]{:S(2)}, u32[]{:S(2)}) collective-permute-start(f32[384,128]{1,0:T(8,128)} %get-tuple-element.40), channel_id=1, source_target_pairs={{0,1},{1,2},{2,3},{3,0},{4,5},{5,6},{6,7},{7,4},{8,9},{9,10},{10,1... | collective-permute-start | bytes 589832 | tf_op jit(solution)/shard_map/ppermute | solution.py:89
  34.8 3.0 %earlier_frames.5.refs_6_ = f32[192,256]{1,0:T(8,128)} custom-call(bf16[2,192,1792]{2,1,0:T(8,128)(2,1)} %get-tuple-element.35.refs_4_.high_ref, bf16[2,192,1792]{2,1,0:T(8,128)(2,1)} %get-tuple-element.36.refs_5_.low_ref, bf16[1792,256]{1,0:T(8,128)(2,1)} %get-tuple-element.52.refs_0_, bf16[1792,256]{1,0:T(8,128)(2,1)} %get-tuple-element.53.refs_1_), custom_call_target="tpu_custom_call" | custom-call | flops 528482304 | bytes 1048576 | tf_op jit(solution)/shard_map/earlier_frames/pallas_call | solution.py:266
  37.8 0.8 collective-permute-start.7
  39.9 2.7 %frame_step.13 = (f32[384,128]{1,0:T(8,128)}, f32[192,128]{1,0:T(8,128)}, f32[192,128]{1,0:T(8,128)}) custom-call(f32[384,128]{1,0:T(8,128)} %copy-done.5, f32[192,128]{1,0:T(8,128)} %copy-done.17, f32[192,128]{1,0:T(8,128)} %copy-done.19, f32[192,1]{1,0:T(8,128)} %copy.8.refs_3_, bf16[2,192,1792]{2,1,0:T(8,128)(2,1)} %get-tuple-element.35.refs_4_.high_ref, ...), custom_call_target="tpu_custom_call" | custom-call | flops 528482304 | bytes 1048576 | tf_op jit(solution)/shard_map/frame_step/pallas_call | solution.py:231
  42.7 1.1 %collective-permute-start.19 = (f32[384,128]{1,0:T(8,128)}, f32[384,128]{1,0:T(8,128)S(1)}, u32[]{:S(2)}, u32[]{:S(2)}) collective-permute-start(f32[384,128]{1,0:T(8,128)} %get-tuple-element.54), channel_id=1, source_target_pairs={{0,1},{1,2},{2,3},{3,0},{4,5},{5,6},{6,7},{7,4},{8,9},{9,10},{10,1... | collective-permute-start | bytes 589832 | tf_op jit(solution)/shard_map/ppermute | solution.py:89
  44.2 1.1 %collective-permute-start.21 = (f32[192,128]{1,0:T(8,128)}, f32[192,128]{1,0:T(8,128)S(1)}, u32[]{:S(2)}, u32[]{:S(2)}) collective-permute-start(f32[192,128]{1,0:T(8,128)} %get-tuple-element.56), channel_id=1, source_target_pairs={{0,1},{1,2},{2,3},{3,0},{4,5},{5,10},{6,7},{7,4},{8,9},{9,6},{10,1... | collective-permute-start | bytes 294920 | tf_op jit(solution)/shard_map/ppermute | solution.py:89
  46.6 3.4 %frame_step.10 = (f32[384,128]{1,0:T(8,128)}, f32[192,128]{1,0:T(8,128)}, f32[192,128]{1,0:T(8,128)}, bf16[1792,256]{1,0:T(8,128)(2,1)}, bf16[1792,256]{1,0:T(8,128)(2,1)}) custom-call(f32[384,128]{1,0:T(8,128)} %copy-done.1, f32[192,128]{1,0:T(8,128)} %copy-done.9, f32[192,128]{1,0:T(8,128)} %copy-done.12, f32[192,1]{1,0:T(8,128)} %copy.8.refs_3_, ...), custom_call_target="tpu_custom_call" | custom-call | flops 528482304 | bytes 1048576 | tf_op jit(solution)/shard_map/frame_step/pallas_call | solution.py:231
  50.5 3.0 %earlier_frames.6.refs_6_ = f32[192,256]{1,0:T(8,128)} custom-call(bf16[2,192,1792]{2,1,0:T(8,128)(2,1)} %get-tuple-element.35.refs_4_.high_ref, bf16[2,192,1792]{2,1,0:T(8,128)(2,1)} %get-tuple-element.36.refs_5_.low_ref, bf16[1792,256]{1,0:T(8,128)(2,1)} %get-tuple-element.57.refs_0_, bf16[1792,256]{1,0:T(8,128)(2,1)} %get-tuple-element.58.refs_1_), custom_call_target="tpu_custom_call" | custom-call | flops 528482304 | bytes 1048576 | tf_op jit(solution)/shard_map/earlier_frames/pallas_call | solution.py:266
  54.9 2.7 %frame_step.14 = (f32[384,128]{1,0:T(8,128)}, f32[192,128]{1,0:T(8,128)}, f32[192,128]{1,0:T(8,128)}) custom-call(f32[384,128]{1,0:T(8,128)} %copy-done.6, f32[192,128]{1,0:T(8,128)} %copy-done.18, f32[192,128]{1,0:T(8,128)} %copy-done.20, f32[192,1]{1,0:T(8,128)} %copy.8.refs_3_, bf16[2,192,1792]{2,1,0:T(8,128)(2,1)} %get-tuple-element.35.refs_4_.high_ref, ...), custom_call_target="tpu_custom_call" | custom-call | flops 528482304 | bytes 1048576 | tf_op jit(solution)/shard_map/frame_step/pallas_call | solution.py:231
  59.3 0.7 copy-done
  60.0 3.4 %frame_step.11 = (f32[384,128]{1,0:T(8,128)}, f32[192,128]{1,0:T(8,128)}, f32[192,128]{1,0:T(8,128)}, bf16[1792,256]{1,0:T(8,128)(2,1)}, bf16[1792,256]{1,0:T(8,128)(2,1)}) custom-call(f32[384,128]{1,0:T(8,128)} %copy-done, f32[192,128]{1,0:T(8,128)} %copy-done.7, f32[192,128]{1,0:T(8,128)} %copy-done.8, f32[192,1]{1,0:T(8,128)} %copy.8.refs_3_, ...), custom_call_target="tpu_custom_call" | custom-call | flops 528482304 | bytes 1048576 | tf_op jit(solution)/shard_map/frame_step/pallas_call | solution.py:231
  63.3 3.0 %earlier_frames.7.refs_6_ = f32[192,256]{1,0:T(8,128)} custom-call(bf16[2,192,1792]{2,1,0:T(8,128)(2,1)} %get-tuple-element.35.refs_4_.high_ref, bf16[2,192,1792]{2,1,0:T(8,128)(2,1)} %get-tuple-element.36.refs_5_.low_ref, bf16[1792,256]{1,0:T(8,128)(2,1)} %get-tuple-element.62.refs_0_, bf16[1792,256]{1,0:T(8,128)(2,1)} %get-tuple-element.63.refs_1_), custom_call_target="tpu_custom_call" | custom-call | flops 528482304 | bytes 1048576 | tf_op jit(solution)/shard_map/earlier_frames/pallas_call | solution.py:266
  67.7 2.7 %frame_step.15 = (f32[384,128]{1,0:T(8,128)}, f32[192,128]{1,0:T(8,128)}, f32[192,128]{1,0:T(8,128)}) custom-call(f32[384,128]{1,0:T(8,128)} %copy-done.4, f32[192,128]{1,0:T(8,128)} %copy-done.21, f32[192,128]{1,0:T(8,128)} %copy-done.22, f32[192,1]{1,0:T(8,128)} %copy.8.refs_3_, bf16[2,192,1792]{2,1,0:T(8,128)(2,1)} %get-tuple-element.35.refs_4_.high_ref, ...), custom_call_target="tpu_custom_call" | custom-call | flops 528482304 | bytes 1048576 | tf_op jit(solution)/shard_map/frame_step/pallas_call | solution.py:231
  70.4 0.9 fusion.8
  71.4 8.0 %collective-permute-start.26 = (f32[96,128]{1,0:T(8,128)S(1)}, f32[96,128]{1,0:T(8,128)S(1)}, u32[]{:S(2)}, u32[]{:S(2)}) collective-permute-start(f32[96,128]{1,0:T(8,128)S(1)} %bitcast.46), channel_id=1, source_target_pairs={{0,2},{1,0},{2,3},{3,1},{4,6},{5,4},{6,7},{7,5},{8,10},{9,8},{10,1... | collective-permute-start | bytes 147464 | tf_op jit(solution)/shard_map/ppermute | solution.py:89
  79.6 2.0 %collective-permute-start.12 = (f32[96,128]{1,0:T(8,128)S(1)}, f32[96,128]{1,0:T(8,128)S(1)}, u32[]{:S(2)}, u32[]{:S(2)}) collective-permute-start(f32[96,128]{1,0:T(8,128)S(1)} %bitcast.47), channel_id=1, source_target_pairs={{0,2},{1,0},{2,3},{3,1},{4,6},{5,4},{6,7},{7,5},{8,10},{9,8},{10,1... | collective-permute-start | bytes 147464 | tf_op jit(solution)/shard_map/ppermute | solution.py:89
  81.6 1.3 %collective-permute-done.27 = f32[96,128]{1,0:T(8,128)S(1)} collective-permute-done((f32[96,128]{1,0:T(8,128)S(1)}, f32[96,128]{1,0:T(8,128)S(1)}, u32[]{:S(2)}, u32[]{:S(2)}) %collective-permute-start.27) | collective-permute-done | bytes 49184 | tf_op jit(solution)/shard_map/ppermute | solution.py:89
  82.9 0.8 fusion.2
  83.7 1.4 %collective-permute-done.13 = f32[96,128]{1,0:T(8,128)S(1)} collective-permute-done((f32[96,128]{1,0:T(8,128)S(1)}, f32[96,128]{1,0:T(8,128)S(1)}, u32[]{:S(2)}, u32[]{:S(2)}) %collective-permute-start.13) | collective-permute-done | bytes 49184 | tf_op jit(solution)/shard_map/ppermute | solution.py:89
  85.1 0.7 copy.16
  (99 shorter events, 10.8 us)
Async XLA Ops:
  0.0 8.1 %copy-start.23 = (f32[1,192]{1,0:T(1,128)S(1)}, f32[1,192]{1,0:T(1,128)}, u32[]{:S(2)}) copy-start(f32[1,192]{1,0:T(1,128)} %param.5) | copy-start | bytes 2308
  1.1 22.3 %collective-permute-start.14 = (f32[192,128]{1,0:T(8,128)S(1)}, f32[192,128]{1,0:T(8,128)S(1)}, u32[]{:S(2)}, u32[]{:S(2)}) collective-permute-start(f32[192,128]{1,0:T(8,128)S(1)} %get-tuple-element.66), channel_id=1, source_target_pairs={{0,4},{1,2},{2,3},{3,1},{4,0},{5,6},{6,7},{7,5},{8,12},{9,10},{10,... | collective-permute-start | bytes 294920 | tf_op jit(solution)/shard_map/ppermute | solution.py:89
  4.2 19.2 %collective-permute-start.15 = (f32[192,128]{1,0:T(8,128)S(1)}, f32[192,128]{1,0:T(8,128)S(1)}, u32[]{:S(2)}, u32[]{:S(2)}) collective-permute-start(f32[192,128]{1,0:T(8,128)S(1)} %get-tuple-element.67), channel_id=1, source_target_pairs={{0,1},{1,0},{2,3},{3,2},{4,8},{5,6},{6,7},{7,5},{8,4},{9,10},{10,1... | collective-permute-start | bytes 294920 | tf_op jit(solution)/shard_map/ppermute | solution.py:89
  4.2 8.6 %collective-permute-start = (f32[192,128]{1,0:T(8,128)S(1)}, f32[192,128]{1,0:T(8,128)S(1)}, u32[]{:S(2)}, u32[]{:S(2)}) collective-permute-start(f32[192,128]{1,0:T(8,128)S(1)} %get-tuple-element.68), channel_id=1, source_target_pairs={{0,4},{1,2},{2,3},{3,1},{4,0},{5,6},{6,7},{7,5},{8,12},{9,10},{10,... | collective-permute-start | bytes 294920 | tf_op jit(solution)/shard_map/ppermute | solution.py:89
  7.3 5.5 %collective-permute-start.1 = (f32[192,128]{1,0:T(8,128)S(1)}, f32[192,128]{1,0:T(8,128)S(1)}, u32[]{:S(2)}, u32[]{:S(2)}) collective-permute-start(f32[192,128]{1,0:T(8,128)S(1)} %get-tuple-element.65), channel_id=1, source_target_pairs={{0,1},{1,0},{2,3},{3,2},{4,8},{5,6},{6,7},{7,5},{8,4},{9,10},{10,1... | collective-permute-start | bytes 294920 | tf_op jit(solution)/shard_map/ppermute | solution.py:89
  18.0 10.5 %collective-permute-start.2 = (f32[384,128]{1,0:T(8,128)}, f32[384,128]{1,0:T(8,128)S(1)}, u32[]{:S(2)}, u32[]{:S(2)}) collective-permute-start(f32[384,128]{1,0:T(8,128)} %get-tuple-element.37), channel_id=1, source_target_pairs={{0,1},{1,0},{2,3},{3,2},{4,5},{5,4},{6,7},{7,6},{8,9},{9,8},{10,11... | collective-permute-start | bytes 589832 | tf_op jit(solution)/shard_map/ppermute | solution.py:89
  18.0 10.4 %collective-permute-start.3 = (f32[192,128]{1,0:T(8,128)}, f32[192,128]{1,0:T(8,128)S(1)}, u32[]{:S(2)}, u32[]{:S(2)}) collective-permute-start(f32[192,128]{1,0:T(8,128)} %get-tuple-element.38), channel_id=1, source_target_pairs={{0,5},{1,0},{2,3},{3,2},{4,1},{5,4},{6,7},{7,6},{8,13},{9,8},{10,1... | collective-permute-start | bytes 294920 | tf_op jit(solution)/shard_map/ppermute | solution.py:89
  19.7 8.7 %collective-permute-start.4 = (f32[192,128]{1,0:T(8,128)}, f32[192,128]{1,0:T(8,128)S(1)}, u32[]{:S(2)}, u32[]{:S(2)}) collective-permute-start(f32[192,128]{1,0:T(8,128)} %get-tuple-element.39), channel_id=1, source_target_pairs={{0,1},{1,0},{2,3},{3,2},{4,9},{5,4},{6,7},{7,6},{8,5},{9,8},{10,11... | collective-permute-start | bytes 294920 | tf_op jit(solution)/shard_map/ppermute | solution.py:89
  27.9 10.7 %collective-permute-start.16 = (f32[384,128]{1,0:T(8,128)}, f32[384,128]{1,0:T(8,128)S(1)}, u32[]{:S(2)}, u32[]{:S(2)}) collective-permute-start(f32[384,128]{1,0:T(8,128)} %get-tuple-element.49), channel_id=1, source_target_pairs={{0,1},{1,0},{2,3},{3,2},{4,5},{5,4},{6,7},{7,6},{8,9},{9,8},{10,11... | collective-permute-start | bytes 589832 | tf_op jit(solution)/shard_map/ppermute | solution.py:89
  27.9 9.9 %collective-permute-start.17 = (f32[192,128]{1,0:T(8,128)}, f32[192,128]{1,0:T(8,128)S(1)}, u32[]{:S(2)}, u32[]{:S(2)}) collective-permute-start(f32[192,128]{1,0:T(8,128)} %get-tuple-element.50), channel_id=1, source_target_pairs={{0,5},{1,0},{2,3},{3,2},{4,1},{5,4},{6,7},{7,6},{8,13},{9,8},{10,1... | collective-permute-start | bytes 294920 | tf_op jit(solution)/shard_map/ppermute | solution.py:89
  28.4 10.2 %collective-permute-start.18 = (f32[192,128]{1,0:T(8,128)}, f32[192,128]{1,0:T(8,128)S(1)}, u32[]{:S(2)}, u32[]{:S(2)}) collective-permute-start(f32[192,128]{1,0:T(8,128)} %get-tuple-element.51), channel_id=1, source_target_pairs={{0,1},{1,0},{2,3},{3,2},{4,9},{5,4},{6,7},{7,6},{8,5},{9,8},{10,11... | collective-permute-start | bytes 294920 | tf_op jit(solution)/shard_map/ppermute | solution.py:89
  33.2 12.0 %collective-permute-start.5 = (f32[384,128]{1,0:T(8,128)}, f32[384,128]{1,0:T(8,128)S(1)}, u32[]{:S(2)}, u32[]{:S(2)}) collective-permute-start(f32[384,128]{1,0:T(8,128)} %get-tuple-element.40), channel_id=1, source_target_pairs={{0,1},{1,2},{2,3},{3,0},{4,5},{5,6},{6,7},{7,4},{8,9},{9,10},{10,1... | collective-permute-start | bytes 589832 | tf_op jit(solution)/shard_map/ppermute | solution.py:89
  34.8 9.4 %collective-permute-start.6 = (f32[192,128]{1,0:T(8,128)}, f32[192,128]{1,0:T(8,128)S(1)}, u32[]{:S(2)}, u32[]{:S(2)}) collective-permute-start(f32[192,128]{1,0:T(8,128)} %get-tuple-element.41), channel_id=1, source_target_pairs={{0,1},{1,6},{2,3},{3,0},{4,5},{5,2},{6,7},{7,4},{8,9},{9,14},{10,1... | collective-permute-start | bytes 294920 | tf_op jit(solution)/shard_map/ppermute | solution.py:89
  34.8 3.0 %copy-start.25 = (f32[192,128]{1,0:T(8,128)S(1)}, f32[192,128]{1,0:T(8,128)}, u32[]{:S(2)}) copy-start(f32[192,128]{1,0:T(8,128)} %get-tuple-element.42) | copy-start | bytes 294916
  37.8 7.4 %collective-permute-start.7 = (f32[192,128]{1,0:T(8,128)S(1)}, f32[192,128]{1,0:T(8,128)S(1)}, u32[]{:S(2)}, u32[]{:S(2)}) collective-permute-start(f32[192,128]{1,0:T(8,128)S(1)} %copy-done.25), channel_id=1, source_target_pairs={{0,1},{1,2},{2,3},{3,0},{4,5},{5,10},{6,7},{7,4},{8,9},{9,6},{10,1... | collective-permute-start | bytes 294920 | tf_op jit(solution)/shard_map/ppermute | solution.py:89
  42.7 10.9 %collective-permute-start.19 = (f32[384,128]{1,0:T(8,128)}, f32[384,128]{1,0:T(8,128)S(1)}, u32[]{:S(2)}, u32[]{:S(2)}) collective-permute-start(f32[384,128]{1,0:T(8,128)} %get-tuple-element.54), channel_id=1, source_target_pairs={{0,1},{1,2},{2,3},{3,0},{4,5},{5,6},{6,7},{7,4},{8,9},{9,10},{10,1... | collective-permute-start | bytes 589832 | tf_op jit(solution)/shard_map/ppermute | solution.py:89
  43.8 9.7 %collective-permute-start.20 = (f32[192,128]{1,0:T(8,128)}, f32[192,128]{1,0:T(8,128)S(1)}, u32[]{:S(2)}, u32[]{:S(2)}) collective-permute-start(f32[192,128]{1,0:T(8,128)} %get-tuple-element.55), channel_id=1, source_target_pairs={{0,1},{1,6},{2,3},{3,0},{4,5},{5,2},{6,7},{7,4},{8,9},{9,14},{10,1... | collective-permute-start | bytes 294920 | tf_op jit(solution)/shard_map/ppermute | solution.py:89
  44.2 9.4 %collective-permute-start.21 = (f32[192,128]{1,0:T(8,128)}, f32[192,128]{1,0:T(8,128)S(1)}, u32[]{:S(2)}, u32[]{:S(2)}) collective-permute-start(f32[192,128]{1,0:T(8,128)} %get-tuple-element.56), channel_id=1, source_target_pairs={{0,1},{1,2},{2,3},{3,0},{4,5},{5,10},{6,7},{7,4},{8,9},{9,6},{10,1... | collective-permute-start | bytes 294920 | tf_op jit(solution)/shard_map/ppermute | solution.py:89
  50.0 8.6 %collective-permute-start.8 = (f32[384,128]{1,0:T(8,128)}, f32[384,128]{1,0:T(8,128)S(1)}, u32[]{:S(2)}, u32[]{:S(2)}) collective-permute-start(f32[384,128]{1,0:T(8,128)} %get-tuple-element.43), channel_id=1, source_target_pairs={{0,1},{1,0},{2,3},{3,2},{4,5},{5,4},{6,7},{7,6},{8,9},{9,8},{10,11... | collective-permute-start | bytes 589832 | tf_op jit(solution)/shard_map/ppermute | solution.py:89
  50.0 8.1 %collective-permute-start.9 = (f32[192,128]{1,0:T(8,128)}, f32[192,128]{1,0:T(8,128)S(1)}, u32[]{:S(2)}, u32[]{:S(2)}) collective-permute-start(f32[192,128]{1,0:T(8,128)} %get-tuple-element.44), channel_id=1, source_target_pairs={{0,1},{1,0},{2,7},{3,2},{4,5},{5,4},{6,3},{7,6},{8,9},{9,8},{10,15... | collective-permute-start | bytes 294920 | tf_op jit(solution)/shard_map/ppermute | solution.py:89
  50.5 3.0 %copy-start.24 = (f32[192,128]{1,0:T(8,128)S(1)}, f32[192,128]{1,0:T(8,128)}, u32[]{:S(2)}) copy-start(f32[192,128]{1,0:T(8,128)} %get-tuple-element.45) | copy-start | bytes 294916
  53.5 5.1 %collective-permute-start.10 = (f32[192,128]{1,0:T(8,128)S(1)}, f32[192,128]{1,0:T(8,128)S(1)}, u32[]{:S(2)}, u32[]{:S(2)}) collective-permute-start(f32[192,128]{1,0:T(8,128)S(1)} %copy-done.24), channel_id=1, source_target_pairs={{0,1},{1,0},{2,3},{3,2},{4,5},{5,4},{6,11},{7,6},{8,9},{9,8},{10,7... | collective-permute-start | bytes 294920 | tf_op jit(solution)/shard_map/ppermute | solution.py:89
  57.6 8.7 %collective-permute-start.22 = (f32[384,128]{1,0:T(8,128)}, f32[384,128]{1,0:T(8,128)S(1)}, u32[]{:S(2)}, u32[]{:S(2)}) collective-permute-start(f32[384,128]{1,0:T(8,128)} %get-tuple-element.59), channel_id=1, source_target_pairs={{0,1},{1,0},{2,3},{3,2},{4,5},{5,4},{6,7},{7,6},{8,9},{9,8},{10,11... | collective-permute-start | bytes 589832 | tf_op jit(solution)/shard_map/ppermute | solution.py:89
  58.1 8.2 %collective-permute-start.23 = (f32[192,128]{1,0:T(8,128)}, f32[192,128]{1,0:T(8,128)S(1)}, u32[]{:S(2)}, u32[]{:S(2)}) collective-permute-start(f32[192,128]{1,0:T(8,128)} %get-tuple-element.60), channel_id=1, source_target_pairs={{0,1},{1,0},{2,7},{3,2},{4,5},{5,4},{6,3},{7,6},{8,9},{9,8},{10,15... | collective-permute-start | bytes 294920 | tf_op jit(solution)/shard_map/ppermute | solution.py:89
  58.1 8.2 %collective-permute-start.24 = (f32[192,128]{1,0:T(8,128)}, f32[192,128]{1,0:T(8,128)S(1)}, u32[]{:S(2)}, u32[]{:S(2)}) collective-permute-start(f32[192,128]{1,0:T(8,128)} %get-tuple-element.61), channel_id=1, source_target_pairs={{0,1},{1,0},{2,3},{3,2},{4,5},{5,4},{6,11},{7,6},{8,9},{9,8},{10,7... | collective-permute-start | bytes 294920 | tf_op jit(solution)/shard_map/ppermute | solution.py:89
  66.3 13.0 %copy-start.3 = (f32[384,128]{1,0:T(8,128)S(1)}, f32[384,128]{1,0:T(8,128)}, u32[]{:S(2)}) copy-start(f32[384,128]{1,0:T(8,128)} %get-tuple-element.46) | copy-start | bytes 589828
  71.3 10.3 %collective-permute-start.25 = (f32[96,128]{1,0:T(8,128)S(1)}, f32[96,128]{1,0:T(8,128)S(1)}, u32[]{:S(2)}, u32[]{:S(2)}) collective-permute-start(f32[96,128]{1,0:T(8,128)S(1)} %bitcast.49), channel_id=1, source_target_pairs={{0,1},{1,0},{2,3},{3,2},{4,5},{5,4},{6,7},{7,6},{8,9},{9,8},{10,11... | collective-permute-start | bytes 147464 | tf_op jit(solution)/shard_map/ppermute | solution.py:89
  71.4 10.2 %collective-permute-start.26 = (f32[96,128]{1,0:T(8,128)S(1)}, f32[96,128]{1,0:T(8,128)S(1)}, u32[]{:S(2)}, u32[]{:S(2)}) collective-permute-start(f32[96,128]{1,0:T(8,128)S(1)} %bitcast.46), channel_id=1, source_target_pairs={{0,2},{1,0},{2,3},{3,1},{4,6},{5,4},{6,7},{7,5},{8,10},{9,8},{10,1... | collective-permute-start | bytes 147464 | tf_op jit(solution)/shard_map/ppermute | solution.py:89
  79.3 3.5 %collective-permute-start.27 = (f32[96,128]{1,0:T(8,128)S(1)}, f32[96,128]{1,0:T(8,128)S(1)}, u32[]{:S(2)}, u32[]{:S(2)}) collective-permute-start(f32[96,128]{1,0:T(8,128)S(1)} %bitcast.44), channel_id=1, source_target_pairs={{0,1},{1,2},{2,3},{3,0},{4,5},{5,6},{6,7},{7,4},{8,9},{9,10},{10,1... | collective-permute-start | bytes 147464 | tf_op jit(solution)/shard_map/ppermute | solution.py:89
  79.4 4.3 %collective-permute-start.11 = (f32[96,128]{1,0:T(8,128)S(1)}, f32[96,128]{1,0:T(8,128)S(1)}, u32[]{:S(2)}, u32[]{:S(2)}) collective-permute-start(f32[96,128]{1,0:T(8,128)S(1)} %bitcast.48), channel_id=1, source_target_pairs={{0,1},{1,0},{2,3},{3,2},{4,5},{5,4},{6,7},{7,6},{8,9},{9,8},{10,11... | collective-permute-start | bytes 147464 | tf_op jit(solution)/shard_map/ppermute | solution.py:89
  79.6 4.1 %collective-permute-start.12 = (f32[96,128]{1,0:T(8,128)S(1)}, f32[96,128]{1,0:T(8,128)S(1)}, u32[]{:S(2)}, u32[]{:S(2)}) collective-permute-start(f32[96,128]{1,0:T(8,128)S(1)} %bitcast.47), channel_id=1, source_target_pairs={{0,2},{1,0},{2,3},{3,1},{4,6},{5,4},{6,7},{7,5},{8,10},{9,8},{10,1... | collective-permute-start | bytes 147464 | tf_op jit(solution)/shard_map/ppermute | solution.py:89
  81.6 3.5 %collective-permute-start.13 = (f32[96,128]{1,0:T(8,128)S(1)}, f32[96,128]{1,0:T(8,128)S(1)}, u32[]{:S(2)}, u32[]{:S(2)}) collective-permute-start(f32[96,128]{1,0:T(8,128)S(1)} %bitcast.45), channel_id=1, source_target_pairs={{0,1},{1,2},{2,3},{3,0},{4,5},{5,6},{6,7},{7,4},{8,9},{9,10},{10,1... | collective-permute-start | bytes 147464 | tf_op jit(solution)/shard_map/ppermute | solution.py:89
  (22 other events, 14.9 us)
